TPU v7x, 32 devices: a whole 2x2x4 slice. The times are simulated.
32 devices in a mesh: tm: 4 (over z), gx: 2 (over y), gy: 4 (over x, core).
Axes of the slice: x: 2, y: 2, z: 4, core: 2. Of those that a mesh axis runs over, the one named last changes fastest.
Arguments:
- segment_opening_values: float32 [4, 4, 24, 64, 128], P('tm', None, 'gx', 'gy'), may hold values from -6 to 6
- cell_material_label: int32 [24, 64, 128], P('gx', 'gy'), may hold values from 0 to 5
- material_rigidity: float32 [6], replicated, may hold values from 0.3 to 3
- dilation_mismatch: float32 [6], replicated, may hold values from -1 to 1
- heat_swings_array: float32 [4, 2], P('tm'), may hold values from 0.5 to 4
- prony_coefficients: float32 [3], replicated, may hold values from 0.2 to 2
- prony_decay_times: float32 [3], replicated, may hold values from 0.7 to 48
Outputs:
- end_state: float32 [4, 4, 24, 64, 128], P('tm', None, 'gx', 'gy')
All inputs are finite; a program needn't handle non-finite values.
Results may differ from a plain program's by a relative error of at most 0.0001.
Values sent between devices are 32-bit elements; how exact they have to be, the bound alone decides.
A program may use at most 64 MiB of HBM per device.

v0:
```python
import functools

import jax
import jax.numpy as jnp
from jax import lax
from jax.experimental import pallas as pl
from jax.experimental.pallas import tpu as pltpu
from jax.sharding import PartitionSpec as P

PARTITION_PACES = 2
SHARP_SOLVER_ITER = 3
LOOSE_SOLVER_ITER = 2
MESH = pl.DeviceIdType.MESH
F32 = jnp.float32
PAD = 8
UNROLL = 4

LAB, U0, H1, HC, HD, U1, HCP, EU = range(8)
N_HALO = 8
FINE_RIM, LOOSE_RIM = SHARP_SOLVER_ITER + 1, LOOSE_SOLVER_ITER + 1
RIM = {
    LAB: FINE_RIM,
    U0: FINE_RIM,
    H1: FINE_RIM - 1,
    HC: LOOSE_RIM - 1,
    HD: FINE_RIM - 1,
    U1: FINE_RIM,
    HCP: LOOSE_RIM - 1,
    EU: LOOSE_RIM,
}
R_FINE1, R_COARSE, R_FINE2, R_CHAIN = range(4)


def chunks_of(nx):
    middle = nx - 2 * LOOSE_RIM
    cut = [(0, LOOSE_RIM), (nx - LOOSE_RIM, LOOSE_RIM)]
    half = middle // 2
    cut += [(LOOSE_RIM, half), (LOOSE_RIM + half, middle - half)]
    return [(start, count) for start, count in cut if count > 0]


def loop(low, high, body, carry):
    return lax.fori_loop(low, high, body, carry, unroll=UNROLL)


def kernel(
    sizes,
    state,
    labels,
    rigidity,
    mismatch,
    heat,
    coefs,
    times,
    out,
    lab_x,
    fields,
    kel_b,
    thermal_b,
    sdiag_b,
    inv_fine,
    inv_loose,
    image_b,
    basis,
    basis_loose,
    part,
    red,
    p_in,
    p_out,
    eu_out,
    u2_b,
    corr_b,
    halo_send,
    halo_recv,
    red_send,
    red_recv,
    tm_send,
    tm_recv,
    side_send,
    side_recv,
):
    n_tm, n_gx, n_gy = sizes
    _, prony, nx, ny, nz = state.shape
    prony -= 1
    h = SHARP_SOLVER_ITER + 1
    rows = nx + 2 * h
    wide = ny + 2 * PAD
    tm, gx, gy = lax.axis_index("tm"), lax.axis_index("gx"), lax.axis_index("gy")
    me = gx * n_gy + gy
    own_r = pl.ds(h, nx)
    own_c = pl.ds(PAD, ny)

    def ext(which):
        return lab_x if which == LAB else fields.at[which - 1]

    lab_x[...] = jnp.full(lab_x.shape, -1, jnp.int32)
    zero_row = jnp.zeros((wide, nz), F32)

    def clear(i, carry):
        for which in range(1, N_HALO):
            fields[which - 1, i] = zero_row
        return carry

    loop(0, rows, clear, 0)
    for row in (h - 1, h + nx):
        for k in range(SHARP_SOLVER_ITER):
            basis[k, row] = zero_row
        for k in range(LOOSE_SOLVER_ITER):
            basis_loose[k, row] = zero_row

    barrier = pltpu.get_barrier_semaphore()
    peers = [(a, b) for a in range(n_gx) for b in range(n_gy)]
    for a, b in peers:

        @pl.when(a * n_gy + b != me)
        def _():
            pl.semaphore_signal(barrier, inc=1, device_id=(tm, a, b), device_id_type=MESH)

    for step in (-1, 1):

        @pl.when((tm + step >= 0) & (tm + step < n_tm))
        def _():
            pl.semaphore_signal(
                barrier, inc=1, device_id=(tm + step, gx, gy), device_id_type=MESH
            )

    def splat(value):
        return jnp.full((1, nz), value, F32)

    def decays(dt):
        decay = [jnp.exp(-dt / splat(times[p])) for p in range(prony)]
        factor = [splat(coefs[p]) * decay[p] for p in range(prony)]
        return decay, factor

    fine_dt, loose_dt = 1.0, 1.0 * PARTITION_PACES
    d_fine, f_fine = decays(fine_dt)
    d_loose, f_loose = decays(loose_dt)
    s_fine = sum(f_fine, splat(1.0 / fine_dt))
    s_loose = sum(f_loose, splat(1.0 / loose_dt))

    def fill(i, carry):
        lab_x[h + i, own_c] = labels[i]
        hist = [state[0, 1 + p, i] for p in range(prony)]
        fields[U0 - 1, h + i, own_c] = state[0, 0, i]
        fields[H1 - 1, h + i, own_c] = sum(f_fine[p] * hist[p] for p in range(prony))
        fields[HC - 1, h + i, own_c] = sum(f_loose[p] * hist[p] for p in range(prony))
        fields[HD - 1, h + i, own_c] = sum(
            f_fine[p] * d_fine[p] * hist[p] for p in range(prony)
        )
        return carry

    loop(0, nx, fill, 0)
    waits = (
        len(peers)
        - 1
        + jnp.where(tm > 0, 1, 0).astype(jnp.int32)
        + jnp.where(tm < n_tm - 1, 1, 0).astype(jnp.int32)
    )
    pl.semaphore_wait(barrier, waits)

    directions = [(a, b) for a in (-1, 0, 1) for b in (-1, 0, 1) if (a, b) != (0, 0)]

    def src_r(a, w):
        return {-1: pl.ds(h, w), 0: own_r, 1: pl.ds(h + nx - w, w)}[a]

    def dst_r(a, w):
        return {-1: pl.ds(h + nx, w), 0: own_r, 1: pl.ds(h - w, w)}[a]

    src_c = {-1: pl.ds(PAD, PAD), 0: own_c, 1: pl.ds(ny, PAD)}
    dst_c = {-1: pl.ds(PAD + ny, PAD), 0: own_c, 1: pl.ds(0, PAD)}

    def exists(a, b):
        return (gx + a >= 0) & (gx + a < n_gx) & (gy + b >= 0) & (gy + b < n_gy)

    def halo_copy(which, index):
        a, b = directions[index]
        ref = ext(which)
        return pltpu.make_async_remote_copy(
            src_ref=ref.at[src_r(a, RIM[which]), src_c[b]],
            dst_ref=ref.at[dst_r(a, RIM[which]), dst_c[b]],
            send_sem=halo_send.at[which, index],
            recv_sem=halo_recv.at[which, index],
            device_id=(tm, gx + a, gy + b),
            device_id_type=MESH,
        )

    def halo_start(*which_all):
        for index, (a, b) in enumerate(directions):

            @pl.when(exists(a, b))
            def _():
                for which in which_all:
                    halo_copy(which, index).start()

    def halo_wait(*which_all):
        for index, (a, b) in enumerate(directions):

            @pl.when(exists(-a, -b))
            def _():
                for which in which_all:
                    halo_copy(which, index).wait_recv()

    def halo_drain(*which_all):
        for index, (a, b) in enumerate(directions):

            @pl.when(exists(a, b))
            def _():
                for which in which_all:
                    halo_copy(which, index).wait_send()

    halo_start(LAB)
    halo_start(U0)
    halo_start(H1)
    halo_start(HC)
    halo_start(HD)

    def red_copy(which, target):
        a, b = peers[target]
        return pltpu.make_async_remote_copy(
            src_ref=part.at[which],
            dst_ref=red.at[which, me],
            send_sem=red_send.at[which, target],
            recv_sem=red_recv.at[which, me],
            device_id=(tm, a, b),
            device_id_type=MESH,
        )

    def red_start(which, sums):
        for j, value in enumerate(sums):
            part[which, j : j + 1] = jnp.sum(value, axis=0, keepdims=True)
        for target in range(len(peers)):

            @pl.when(target != me)
            def _():
                red_copy(which, target).start()

    def red_finish(which, count):
        for source in range(len(peers)):

            @pl.when(source != me)
            def _():
                pltpu.make_async_remote_copy(
                    src_ref=part.at[which],
                    dst_ref=red.at[which, source],
                    send_sem=red_send.at[which, source],
                    recv_sem=red_recv.at[which, source],
                    device_id=(tm, gx, gy),
                    device_id_type=MESH,
                ).wait_recv()

        mine = part[which]
        total = None
        for source in range(len(peers)):
            value = jnp.where(source == me, mine, red[which, source])
            total = value if total is None else total + value
        total = jnp.broadcast_to(jnp.sum(total, axis=1, keepdims=True), total.shape)
        return [total[j : j + 1] for j in range(count)]

    def red_drain(which):
        for target in range(len(peers)):

            @pl.when(target != me)
            def _():
                red_copy(which, target).wait_send()

    lane = lax.broadcasted_iota(jnp.int32, (wide, nz), 1)
    first_lane, last_lane = lane == 0, lane == nz - 1

    def next_z(v):
        return jnp.where(last_lane, 0.0, pltpu.roll(v, nz - 1, 1))

    def prior_z(v):
        return jnp.where(first_lane, 0.0, pltpu.roll(v, 1, 1))

    def next_y(v):
        return pltpu.roll(v, wide - 1, 0)

    def prior_y(v):
        return pltpu.roll(v, 1, 0)

    def forward(v):
        up = next_z(v)
        total, diff = v + up, up - v
        total_up, diff_up = next_y(total), next_y(diff)
        return (total + total_up, diff + diff_up, total_up - total, diff_up - diff)

    def element_row(low, high, k):
        k2 = k + k
        k3 = k2 + k
        g1 = k3 * (high[0] - low[0])
        to_low, to_high = [-g1], [g1]
        for f, weights in ((1, (k3, k2)), (2, (k3, k2)), (3, (k2, k))):
            g0 = weights[0] * (high[f] + low[f])
            g1 = weights[1] * (high[f] - low[f])
            to_low.append(g0 - g1)
            to_high.append(g0 + g1)
        return to_low, to_high

    def backward(g):
        zs = (g[0] - g[2]) + prior_y(g[0] + g[2])
        zd = (g[1] - g[3]) + prior_y(g[1] + g[3])
        return (zs - zd) + prior_z(zs + zd)

    def span(margin):
        if n_gx == 1:
            return h, nx
        if n_gx == 2:
            return h - margin * gx, nx + margin
        return h - margin, nx + 2 * margin

    def apply(load, emit, margin, extra):
        low_row, count = span(margin)
        before = forward(load(low_row - 1))
        here = forward(load(low_row))
        _, pending = element_row(before, here, kel_b[low_row - 1])

        def body(t, carry):
            here, pending, extra = carry
            e = low_row + t
            after = forward(load(e + 1))
            to_low, to_high = element_row(here, after, kel_b[e])
            image = backward([x + y for x, y in zip(pending, to_low)])
            extra = emit(e, image, extra)
            return after, tuple(to_high), extra

        _, _, extra = lax.fori_loop(
            0, count, body, (here, tuple(pending), extra), unroll=True
        )
        return extra

    zero_sum = jnp.zeros((ny, nz), F32)

    def own(v):
        return v[PAD : PAD + ny]

    def own_weight(e):
        return jnp.where((e >= h) & (e < h + nx), 1.0, 0.0).astype(F32)

    def krylov(iterations, basis, inv_b, level0):
        sums = [level0]
        for k in range(iterations):
            final = k + 1 == iterations

            def emit(e, image, carry):
                v = basis[k, e]
                t = image - sdiag_b[e] * v
                if final:
                    return (carry[0] + own(v * t),)
                v_new = inv_b[e] * t
                basis[k + 1, e] = v_new
                w = own_weight(e)
                t = own(t) * w
                return carry[0] + own(v) * t, carry[1] + own(v_new) * t

            count = 1 if final else 2
            got = apply(
                lambda e: basis[k, e], emit, iterations - 1 - k, (zero_sum,) * count
            )
            sums.extend(got)
        return sums

    def first_level(u_ref, h_ref, u_weight, level, inv_b, margin, keep_image):
        def emit(e, image, carry):
            if keep_image:
                image_b[e] = image
            r = u_weight * u_ref[e] + level * thermal_b[e] + h_ref[e] - image
            v = inv_b[e] * r
            basis[0, e] = v
            return (carry[0] + own(v * r) * own_weight(e),)

        return apply(lambda e: u_ref[e], emit, margin, (zero_sum,))[0]

    def guarded(numerator, denominator):
        good = denominator > 0.0
        return jnp.where(good, numerator / jnp.where(good, denominator, 1.0), 0.0)

    def galerkin(nu, m):
        a = [nu[j] + nu[j + 1] for j in range(2 * m - 1)]
        lower = [[None] * m for _ in range(m)]
        pivots, y = [], []
        for i in range(m):
            row = []
            for j in range(i):
                value = a[i + j]
                for q in range(j):
                    value = value - row[q] * lower[j][q]
                row.append(value)
                lower[i][j] = guarded(value, pivots[j])
            pivot, rhs = a[2 * i], nu[i]
            for q in range(i):
                pivot = pivot - row[q] * lower[i][q]
                rhs = rhs - lower[i][q] * y[q]
            pivots.append(pivot)
            y.append(rhs)
        c = [None] * m
        for i in reversed(range(m)):
            value = guarded(y[i], pivots[i])
            for q in range(i + 1, m):
                value = value - lower[q][i] * c[q]
            c[i] = value
        return c

    def solved(u, c, i, basis=basis):
        for k, weight in enumerate(c):
            u = u + weight * basis[k, h + i, own_c]
        return u

    halo_wait(LAB)
    node_y = gy * ny - PAD + lax.broadcasted_iota(jnp.int32, (wide, nz), 0)
    inside_y = (node_y >= 0) & (node_y < n_gy * ny)

    def coefficients(e):
        ids = lab_x[e]
        kel = jnp.zeros((wide, nz), F32)
        gap = jnp.zeros((wide, nz), F32)
        for region in range(rigidity.shape[0]):
            here = ids == region
            kel = jnp.where(here, rigidity[region], kel)
            gap = jnp.where(here, mismatch[region], gap)
        kal = kel * gap
        return kel, kal

    def nodal(kel, kal):
        kel_y = kel + prior_y(kel)
        kal_y = kal + prior_y(kal)
        return kel_y + prior_z(kel_y), prior_z(kal_y) - kal_y

    kel, kal = coefficients(0)
    kel_b[0] = kel * (1.0 / 48.0)

    def setup(e, carry):
        kel, kal = coefficients(e)
        kel_b[e] = kel * (1.0 / 48.0)
        new = nodal(kel, kal)
        diag = (carry[0] + new[0]) * (1.0 / 3.0)
        sdiag_b[e] = diag
        thermal_b[e] = (carry[1] + new[1]) * 0.25
        node_x = gx * nx - h + e
        inside = jnp.where((node_x >= 0) & (node_x < n_gx * nx), 1.0, 0.0).astype(F32)
        inv_fine[e] = jnp.where(inside_y, inside / (s_fine + diag), 0.0)
        inv_loose[e] = jnp.where(inside_y, inside / (s_loose + diag), 0.0)
        return new

    loop(1, rows, setup, nodal(kel, kal))

    heat_fine = [splat(heat[0, s]) for s in range(PARTITION_PACES)]
    heat_loose = heat_fine[PARTITION_PACES - 1]
    u0_x, u1_x, eu_x = ext(U0), ext(U1), ext(EU)

    halo_wait(U0, H1)
    level0 = first_level(
        u0_x,
        ext(H1),
        splat(1.0 / fine_dt) - s_fine,
        heat_fine[0],
        inv_fine,
        SHARP_SOLVER_ITER,
        True,
    )
    red_start(R_FINE1, krylov(SHARP_SOLVER_ITER, basis, inv_fine, level0))

    halo_wait(HC)
    h_coarse = ext(HC)
    coarse_low, coarse_count = span(LOOSE_SOLVER_ITER)

    def coarse_first(t, carry):
        e = coarse_low + t
        r = (
            (splat(1.0 / loose_dt) - s_loose) * u0_x[e]
            + heat_loose * thermal_b[e]
            + h_coarse[e]
            - image_b[e]
        )
        v = inv_loose[e] * r
        basis_loose[0, e] = v
        return carry + own(v * r) * own_weight(e)

    level0 = loop(0, coarse_count, coarse_first, zero_sum)
    red_start(R_COARSE, krylov(LOOSE_SOLVER_ITER, basis_loose, inv_loose, level0))

    c = galerkin(red_finish(R_FINE1, 2 * SHARP_SOLVER_ITER), SHARP_SOLVER_ITER)

    def end_fine1(i, carry):
        fields[U1 - 1, h + i, own_c] = solved(u0_x[h + i, own_c], c, i)
        return carry

    loop(0, nx, end_fine1, 0)
    halo_start(U1)

    keep_fine = [1.0 - d for d in d_fine]
    keep_loose = [1.0 - d for d in d_loose]

    def give_fine(i, carry):
        u1 = u1_x[h + i, own_c]
        for p in range(prony):
            p_out[p, i] = d_fine[p] * (
                d_fine[p] * state[0, 1 + p, i] + keep_fine[p] * u1
            )
        return carry

    loop(0, nx, give_fine, 0)

    chunks = chunks_of(nx)

    def tm_copy(index, up):
        if index < prony:
            src, dst = p_out.at[index], p_in.at[index]
        else:
            start, count = chunks[index - prony]
            src = eu_out.at[pl.ds(start, count)]
            dst = eu_x.at[pl.ds(h + start, count), own_c]
        return pltpu.make_async_remote_copy(
            src_ref=src,
            dst_ref=dst,
            send_sem=tm_send.at[index],
            recv_sem=tm_recv.at[index],
            device_id=(tm + up, gx, gy),
            device_id_type=MESH,
        )

    def side_copy(index, side):
        start, count = chunks[index]
        b = (-1, 1)[side]
        at = pl.ds(h + start, count)
        return pltpu.make_async_remote_copy(
            src_ref=eu_x.at[at, src_c[b]],
            dst_ref=eu_x.at[at, dst_c[b]],
            send_sem=side_send.at[index, side],
            recv_sem=side_recv.at[index, side],
            device_id=(tm, gx, gy + b),
            device_id_type=MESH,
        )

    def end_wait():
        for side, b in enumerate((-1, 1)):

            @pl.when(exists(0, -b))
            def _():
                for index in range(len(chunks)):
                    side_copy(index, side).wait_recv()

        for corner, (a, b) in enumerate(directions):
            if a != 0:

                @pl.when(exists(-a, -b))
                def _():
                    halo_copy(EU, corner).wait_recv()

    def end_drain():
        for side, b in enumerate((-1, 1)):

            @pl.when(exists(0, b))
            def _():
                for index in range(len(chunks)):
                    side_copy(index, side).wait_send()

        for corner, (a, b) in enumerate(directions):
            if a != 0:

                @pl.when(exists(a, b))
                def _():
                    halo_copy(EU, corner).wait_send()

    has_next = tm < n_tm - 1

    @pl.when((tm == 0) & has_next)
    def _():
        for p in range(prony):
            tm_copy(p, 1).start()

    c = galerkin(red_finish(R_COARSE, 2 * LOOSE_SOLVER_ITER), LOOSE_SOLVER_ITER)

    def end_coarse(i, carry):
        u = solved(u0_x[h + i, own_c], c, i, basis_loose)
        corr_b[0, i] = -u
        for p in range(prony):
            corr_b[1 + p, i] = -(d_loose[p] * state[0, 1 + p, i] + keep_loose[p] * u)
        return carry

    loop(0, nx, end_coarse, 0)

    halo_wait(HD, U1)
    held = sum((f_fine[p] * d_fine[p] for p in range(prony)), splat(0.0))
    level0 = first_level(
        u1_x, ext(HD), -held, heat_fine[1], inv_fine, SHARP_SOLVER_ITER, False
    )
    red_start(R_FINE2, krylov(SHARP_SOLVER_ITER, basis, inv_fine, level0))
    c_fine = galerkin(red_finish(R_FINE2, 2 * SHARP_SOLVER_ITER), SHARP_SOLVER_ITER)

    @pl.when(tm == 0)
    def _():
        def first_u(i, carry):
            eu_out[i] = solved(u1_x[h + i, own_c], c_fine, i)
            return carry

        for index, (start, count) in enumerate(chunks):
            loop(start, start + count, first_u, 0)

            @pl.when(has_next)
            def _():
                tm_copy(prony + index, 1).start()

        def first_out(i, carry):
            u2 = eu_out[i]
            out[0, 0, i] = u2
            for p in range(prony):
                out[0, 1 + p, i] = p_out[p, i] + keep_fine[p] * u2
            return carry

        loop(0, nx, first_out, 0)

    @pl.when(tm > 0)
    def _():
        def correct(i, carry):
            u2 = solved(u1_x[h + i, own_c], c_fine, i)
            corr_b[0, i] = corr_b[0, i] + u2
            for p in range(prony):
                corr_b[1 + p, i] = corr_b[1 + p, i] + (p_out[p, i] + keep_fine[p] * u2)
            return carry

        loop(0, nx, correct, 0)

        from_first = tm == 1
        given = [jnp.where(from_first, keep_fine[p], keep_loose[p]) for p in range(prony)]
        for p in range(prony):
            tm_copy(p, -1).wait_recv()

        def combine(i, carry):
            fields[HCP - 1, h + i, own_c] = sum(f_loose[p] * p_in[p, i] for p in range(prony))
            return carry

        loop(0, nx, combine, 0)
        halo_start(HCP)
        for index in range(len(chunks)):
            tm_copy(prony + index, -1).wait_recv()
            for side, b in enumerate((-1, 1)):

                @pl.when(exists(0, b))
                def _():
                    side_copy(index, side).start()

            if index < 2:
                for corner, (a, b) in enumerate(directions):
                    if a == (-1, 1)[index]:

                        @pl.when(exists(a, b))
                        def _():
                            halo_copy(EU, corner).start()

        def ahead(i, carry):
            u = eu_x[h + i, own_c]
            for p in range(prony):
                old = p_in[p, i] + given[p] * u
                p_out[p, i] = (
                    d_loose[p] * old + corr_b[1 + p, i] - keep_loose[p] * corr_b[0, i]
                )
            return carry

        loop(0, nx, ahead, 0)

        @pl.when(has_next)
        def _():
            for p in range(prony):
                tm_copy(p, 1).start()

        halo_wait(HCP)
        end_wait()
        gain = splat(1.0 / loose_dt) - s_loose
        for p in range(prony):
            gain = gain + f_loose[p] * given[p]
        level0 = first_level(
            eu_x, ext(HCP), gain, heat_loose, inv_loose, LOOSE_SOLVER_ITER, False
        )
        red_start(R_CHAIN, krylov(LOOSE_SOLVER_ITER, basis, inv_loose, level0))
        c = galerkin(red_finish(R_CHAIN, 2 * LOOSE_SOLVER_ITER), LOOSE_SOLVER_ITER)

        def last_u(i, carry):
            eu_out[i] = solved(eu_x[h + i, own_c], c, i) + corr_b[0, i]
            return carry

        for index, (start, count) in enumerate(chunks):
            loop(start, start + count, last_u, 0)

            @pl.when(has_next)
            def _():
                tm_copy(prony + index, 1).start()

        def last_out(i, carry):
            u = eu_out[i]
            out[0, 0, i] = u
            for p in range(prony):
                out[0, 1 + p, i] = p_out[p, i] + keep_loose[p] * u
            return carry

        loop(0, nx, last_out, 0)
        halo_drain(HCP)
        end_drain()
        red_drain(R_CHAIN)

    @pl.when(has_next)
    def _():
        for index in range(prony + len(chunks)):
            tm_copy(index, 1).wait_send()

    halo_drain(LAB, U0, H1, HC, HD, U1)
    for which in (R_FINE1, R_COARSE, R_FINE2):
        red_drain(which)


def on_device(sizes, state, labels, rigidity, mismatch, heat, coefs, times):
    _, fields, nx, ny, nz = state.shape
    h = SHARP_SOLVER_ITER + 1
    rows, wide = nx + 2 * h, ny + 2 * PAD
    peers = sizes[1] * sizes[2]
    steps = len(chunks_of(nx))
    field = (rows, wide, nz)
    own = (nx, ny, nz)
    vmem = pl.BlockSpec(memory_space=pltpu.VMEM)
    smem = pl.BlockSpec(memory_space=pltpu.SMEM)
    dma = pltpu.SemaphoreType.DMA
    return pl.pallas_call(
        functools.partial(kernel, sizes),
        out_shape=jax.ShapeDtypeStruct(state.shape, state.dtype),
        in_specs=[vmem, vmem, smem, smem, smem, smem, smem],
        out_specs=vmem,
        scratch_shapes=[
            pltpu.VMEM(field, jnp.int32),
            pltpu.VMEM((N_HALO - 1,) + field, F32),
            pltpu.VMEM(field, F32),
            pltpu.VMEM(field, F32),
            pltpu.VMEM(field, F32),
            pltpu.VMEM(field, F32),
            pltpu.VMEM(field, F32),
            pltpu.VMEM(field, F32),
            pltpu.VMEM((SHARP_SOLVER_ITER,) + field, F32),
            pltpu.VMEM((LOOSE_SOLVER_ITER,) + field, F32),
            pltpu.VMEM((4, 8, nz), F32),
            pltpu.VMEM((4, peers, 8, nz), F32),
            pltpu.VMEM((fields - 1,) + own, F32),
            pltpu.VMEM((fields - 1,) + own, F32),
            pltpu.VMEM(own, F32),
            pltpu.VMEM(own, F32),
            pltpu.VMEM((fields,) + own, F32),
            dma((N_HALO, 8)),
            dma((N_HALO, 8)),
            dma((4, peers)),
            dma((4, peers)),
            dma((fields - 1 + steps,)),
            dma((fields - 1 + steps,)),
            dma((steps, 2)),
            dma((steps, 2)),
        ],
        compiler_params=pltpu.CompilerParams(
            collective_id=0, has_side_effects=True, vmem_limit_bytes=56 * 1024 * 1024
        ),
    )(state, labels, rigidity, mismatch, heat, coefs, times)


def solution(mesh):
    sizes = tuple(mesh.shape[name] for name in ("tm", "gx", "gy"))
    placed = (
        P("tm", None, "gx", "gy", None),
        P("gx", "gy", None),
        P(),
        P(),
        P("tm", None),
        P(),
        P(),
    )
    return jax.shard_map(
        functools.partial(on_device, sizes),
        mesh=mesh,
        in_specs=placed,
        out_specs=P("tm", None, "gx", "gy", None),
        check_vma=False,
    )
```

profile of v0, /device:TPU:25, one launch (start us, length us, event | category | flops | bytes accessed | tf_op | source)
XLA Modules:
  0.0 59.7 jit_solution(9251490253809063080)
XLA Ops:
  0.0 57.9 %shard_map.73 = f32[1,4,12,16,128]{4,3,2,1,0:T(8,128)} custom-call(f32[1,4,12,16,128]{4,3,2,1,0:T(8,128)} %state.1, s32[12,16,128]{2,1,0:T(8,128)} %labels.1, f32[6]{0:T(128)} %rigidity.1, f32[6]{0:T(128)} %mismatch.1, f32[1,2]{1,0:T(1,128)} %heat.1, f32[3]{0:T(128)} %coefs.1, f32[3]{0:T(128)} %times.1), custom_call_target="tpu_custom_call" | custom-call | tf_op jit(solution)/shard_map/pallas_call | solution.py:721
  57.9 1.8 %copy.9 = f32[1,4,12,16,128]{4,3,2,1,0:T(8,128)} copy(f32[1,4,12,16,128]{4,3,2,1,0:T(8,128)} %shard_map.73) | data formatting | bytes 786432
where the time goes:
time: 59.9 us; the launch traced here: 59.7 us
  Pallas kernels  57.9 us (97%)
  local copies, waits for them, and re-layouts  1.77 us (3%)
    pallas_call x1, Pallas kernels, on_device(): pl.pallas_call(functools.partial(kernel, sizes), out_shape=jax.ShapeDtype...  57.9 us
    unnamed x1, local copies, waits for them, and re-layouts  1.77 us

commit v1 on v0

v1 whole, which is shorter than its diff:
```python
import functools

import jax
import jax.numpy as jnp
from jax import lax
from jax.experimental import pallas as pl
from jax.experimental.pallas import tpu as pltpu
from jax.sharding import PartitionSpec as P

PARTITION_PACES = 2
SHARP_SOLVER_ITER = 3
LOOSE_SOLVER_ITER = 2
MESH = pl.DeviceIdType.MESH
F32 = jnp.float32
PAD = 8
SIDE = 4
CHUNKS = 3

MF, ML = SHARP_SOLVER_ITER, LOOSE_SOLVER_ITER
RIM = MF + 1
LAB, U0, H1, HD, HC, HIST = range(6)
R_FINE1, R_COARSE, R_FINE2, R_STAGE = range(4)


def chunks_of(nx):
    cut = [nx * j // CHUNKS for j in range(CHUNKS + 1)]
    return [(a, b - a) for a, b in zip(cut, cut[1:]) if b > a]


def loop(count, body, carry=0, unroll=True):
    return lax.fori_loop(0, count, body, carry, unroll=unroll)


def kernel(
    sizes,
    state,
    labels,
    rigidity,
    mismatch,
    heat,
    coefs,
    times,
    out,
    lab_x,
    in_x,
    k_b,
    kal_b,
    kz_b,
    cx_b,
    cy_b,
    cz_b,
    s8_b,
    theta_b,
    ef_b,
    el_b,
    vf,
    vg,
    vc,
    vs,
    xf,
    xg,
    xs,
    ab,
    au_b,
    rb_b,
    u_b,
    aa_b,
    hb,
    own_ab,
    gu_out,
    gu_in,
    y_out,
    y_in,
    first_in,
    heat_out,
    heat_in,
    part,
    red,
    halo_send,
    halo_recv,
    red_send,
    red_recv,
    z_send,
    z_recv,
    y_send,
    y_recv,
    heat_send,
    heat_recv,
    token,
):
    n_tm, n_gx, n_gy = sizes
    _, prony, nx, ny, nz = state.shape
    prony -= 1
    h = RIM
    wide = ny + 2 * PAD
    span_y = ny + 2 * SIDE
    stages = n_tm - 1
    inner = max(stages - 1, 0)
    tm, gx, gy = lax.axis_index("tm"), lax.axis_index("gx"), lax.axis_index("gy")
    me = gx * n_gy + gy
    n_peer = n_gx * n_gy
    own_r, own_c = pl.ds(h, nx), pl.ds(PAD, ny)
    XF = HIST + prony
    XG = XF + MF
    XS = XG + MF
    AB = XS + ML * inner
    first_plane = tm == 0
    chunks = chunks_of(nx)

    def win(ref, e, shift=0):
        return ref[e, pl.ds(SIDE + shift, span_y)]

    def put(ref, e, value):
        ref[e, pl.ds(SIDE, span_y)] = value

    directions = [(a, b) for a in (-1, 0, 1) for b in (-1, 0, 1) if (a, b) != (0, 0)]
    compass = directions + [(0, 0)]

    def exists(a, b):
        return (gx + a >= 0) & (gx + a < n_gx) & (gy + b >= 0) & (gy + b < n_gy)

    lab_x[...] = jnp.full(lab_x.shape, -1, jnp.int32)

    barrier = pltpu.get_barrier_semaphore()

    def greet(t, a, b):
        pl.semaphore_signal(barrier, inc=1, device_id=(t, a, b), device_id_type=MESH)

    for j in range(1, n_peer):
        peer = lax.rem(me + j, n_peer)
        greet(tm, peer // n_gy, lax.rem(peer, n_gy))

    for step in (-1, 1):

        @pl.when((tm + step >= 0) & (tm + step < n_tm))
        def _():
            greet(tm + step, gx, gy)

    def count_of(flag):
        return jnp.where(flag, 1, 0).astype(jnp.int32)

    cross = count_of(tm > 0) + count_of(tm < n_tm - 1)

    def splat(value):
        return jnp.full((1, nz), value, F32)

    def decays(dt):
        decay = [jnp.exp(-dt / splat(times[p])) for p in range(prony)]
        factor = [splat(coefs[p]) * decay[p] for p in range(prony)]
        return decay, factor

    fine_dt, loose_dt = 1.0, 1.0 * PARTITION_PACES
    d_f, f_f = decays(fine_dt)
    d_l, f_l = decays(loose_dt)
    s_f = sum(f_f, splat(1.0 / fine_dt))
    s_l = sum(f_l, splat(1.0 / loose_dt))
    keep_f = [1.0 - d for d in d_f]
    keep_l = [1.0 - d for d in d_l]
    prods = range(prony)
    held = sum((f_f[p] * d_f[p] for p in prods), splat(0.0))
    kappa_f = sum((f_l[p] * keep_f[p] for p in prods), splat(0.0))
    kappa_l = sum((f_l[p] * keep_l[p] for p in prods), splat(0.0))
    gain_f = 1.0 / fine_dt - s_f
    gain_l = 1.0 / loose_dt - s_l
    heat_f = [splat(heat[0, s]) for s in range(PARTITION_PACES)]
    heat_l = heat_f[PARTITION_PACES - 1]

    def fill(i, carry):
        lab_x[h + i, own_c] = labels[i]
        hist = [state[0, 1 + p, i] for p in prods]
        in_x[U0 - 1, h + i, own_c] = state[0, 0, i]
        in_x[H1 - 1, h + i, own_c] = sum(f_f[p] * hist[p] for p in prods)
        in_x[HD - 1, h + i, own_c] = sum((f_f[p] * d_f[p]) * hist[p] for p in prods)
        in_x[HC - 1, h + i, own_c] = sum(f_l[p] * hist[p] for p in prods)
        for p in prods:
            in_x[HIST - 1 + p, h + i, own_c] = hist[p]
        return carry

    def clear_strips(refs, value, dtype):
        row = jnp.full((wide, nz), value, dtype)
        pad = jnp.full((PAD, nz), value, dtype)
        for flag, start in ((gx == 0, 0), (gx == n_gx - 1, h + nx)):

            @pl.when(flag)
            def _():
                for ref in refs:
                    for i in range(h):
                        ref[start + i] = row

        for flag, start in ((gy == 0, 0), (gy == n_gy - 1, PAD + ny)):

            @pl.when(flag)
            def _():
                def body(i, carry):
                    for ref in refs:
                        ref[i, pl.ds(start, PAD)] = pad
                    return carry

                lax.fori_loop(0, nx + 2 * h, body, 0)

    loop(nx, fill, unroll=4)
    pl.semaphore_wait(barrier, n_peer - 1 + cross)

    def src_r(a, w):
        return {-1: pl.ds(h, w), 0: own_r, 1: pl.ds(h + nx - w, w)}[a]

    def dst_r(a, w):
        return {-1: pl.ds(h + nx, w), 0: own_r, 1: pl.ds(h - w, w)}[a]

    src_c = {-1: pl.ds(PAD, SIDE), 0: own_c, 1: pl.ds(PAD + ny - SIDE, SIDE)}
    dst_c = {-1: pl.ds(PAD + ny, SIDE), 0: own_c, 1: pl.ds(PAD - SIDE, SIDE)}

    def halo_copy(ref, which, rim, index):
        a, b = directions[index]
        return pltpu.make_async_remote_copy(
            src_ref=ref.at[src_r(a, rim), src_c[b]],
            dst_ref=ref.at[dst_r(a, rim), dst_c[b]],
            send_sem=halo_send.at[which, index],
            recv_sem=halo_recv.at[which, index],
            device_id=(tm, gx + a, gy + b),
            device_id_type=MESH,
        )

    def halo_each(messages, sign, act):
        for index, (a, b) in enumerate(directions):

            @pl.when(exists(sign * a, sign * b))
            def _():
                for ref, which, rim in messages:
                    act(halo_copy(ref, which, rim, index))

    def halo_start(*messages):
        halo_each(messages, 1, lambda c: c.start())

    def halo_wait(*messages):
        halo_each(messages, -1, lambda c: c.wait_recv())

    def halo_drain(*messages):
        halo_each(messages, 1, lambda c: c.wait_send())

    def field(which, rim):
        return (lab_x if which == LAB else in_x.at[which - 1], which, rim)

    m_lab, m_u0, m_h1 = field(LAB, RIM), field(U0, RIM), field(H1, MF)
    m_hd, m_hc = field(HD, MF), field(HC, ML)
    m_hist = [field(HIST + p, ML) for p in prods]
    m_xf = [(xf.at[k], XF + k, MF) for k in range(MF)]
    m_xg = [(xg.at[k], XG + k, ML) for k in range(MF)]

    def m_xs(n):
        base = ML * (n - 1)
        return [(xs.at[base + k], XS + base + k, ML) for k in range(ML)]

    def give_copy(n, f, index):
        a, b = compass[index]
        w = ML + 1
        rows = {-1: pl.ds(0, w), 0: pl.ds(0, nx), 1: pl.ds(nx - w, w)}[a]
        cols = {-1: pl.ds(0, SIDE), 0: pl.ds(0, ny), 1: pl.ds(ny - SIDE, SIDE)}[b]
        at = 2 * (n - 1) + f
        return pltpu.make_async_remote_copy(
            src_ref=own_ab.at[f, rows, cols],
            dst_ref=ab.at[at, dst_r(a, w), dst_c[b]],
            send_sem=halo_send.at[AB + at, index],
            recv_sem=halo_recv.at[AB + at, index],
            device_id=(tm - n, gx + a, gy + b),
            device_id_type=MESH,
        )

    def give_each(n, f, sign, act):
        for index, (a, b) in enumerate(compass):

            @pl.when(exists(sign * a, sign * b))
            def _():
                act(give_copy(n, f, index))

    def give(f, act):
        for n in range(1, stages):
            for index, (a, b) in enumerate(compass):

                @pl.when((tm == n) & exists(a, b))
                def _():
                    act(give_copy(n, f, index))

    def heat_copy():
        return pltpu.make_async_remote_copy(
            src_ref=heat_out,
            dst_ref=heat_in,
            send_sem=heat_send,
            recv_sem=heat_recv,
            device_id=(tm - 1, gx, gy),
            device_id_type=MESH,
        )

    def z_items(j):
        if j < stages:
            return [(j - 1, pl.ds(0, nx))]
        return [(stages - 1 + k, pl.ds(*cut)) for k, cut in enumerate(chunks)]

    def z_copies(j, n):
        return [
            pltpu.make_async_remote_copy(
                src_ref=gu_out.at[j - 1, at],
                dst_ref=gu_in.at[j - 1, at],
                send_sem=z_send.at[n - 1, item],
                recv_sem=z_recv.at[item],
                device_id=(tm + n, gx, gy),
                device_id_type=MESH,
            )
            for item, at in z_items(j)
        ]

    def up_copy(item, first):
        if item >= prony:
            src, dst = own_ab.at[item - prony], first_in.at[item - prony]
        else:
            src = state.at[0, 1 + item] if first else y_out.at[item]
            dst = y_in.at[item]
        return pltpu.make_async_remote_copy(
            src_ref=src,
            dst_ref=dst,
            send_sem=y_send.at[item],
            recv_sem=y_recv.at[item],
            device_id=(tm + 1, gx, gy),
            device_id_type=MESH,
        )

    halo_start(m_lab)
    halo_start(m_u0)
    halo_start(m_h1)
    halo_start(m_hd)

    @pl.when(first_plane)
    def _():
        for p in prods:
            up_copy(p, True).start()
        if inner:
            pl.semaphore_signal(
                token, inc=1, device_id=(tm + 1, gx, gy), device_id_type=MESH
            )

    @pl.when(tm > 0)
    def _():
        halo_start(m_hc)

    def heat_relay():
        heat_copy().wait_recv()
        heat_out[...] = heat_in[...]
        heat_out[tm - 1] = jnp.broadcast_to(heat_l, (8, nz))
        heat_copy().start()

    @pl.when(tm == n_tm - 1)
    def _():
        heat_out[...] = jnp.zeros(heat_out.shape, F32)
        heat_out[tm - 1] = jnp.broadcast_to(heat_l, (8, nz))
        heat_copy().start()

    clear_strips([in_x.at[j] for j in range(4 + prony)], 0.0, F32)

    def red_copy(which, j):
        peer = lax.rem(me + j, n_peer)
        return pltpu.make_async_remote_copy(
            src_ref=part.at[which],
            dst_ref=red.at[which, n_peer - 1 - j],
            send_sem=red_send.at[which],
            recv_sem=red_recv.at[which],
            device_id=(tm, peer // n_gy, lax.rem(peer, n_gy)),
            device_id_type=MESH,
        )

    def red_all(which):
        return pltpu.make_async_remote_copy(
            src_ref=red.at[which],
            dst_ref=red.at[which],
            send_sem=red_send.at[which],
            recv_sem=red_recv.at[which],
            device_id=(tm, gx, gy),
            device_id_type=MESH,
        )

    def red_start(which, sums):
        for j, value in enumerate(sums):
            part[which, j : j + 1] = jnp.sum(value, axis=0, keepdims=True)
        for j in range(1, n_peer):
            red_copy(which, j).start()

    def red_finish(which, count):
        if n_peer > 1:
            red_all(which).wait_recv()
        values = [part[which]] + [red[which, j] for j in range(n_peer - 1)]
        while len(values) > 1:
            values = [
                values[i] + values[i + 1] if i + 1 < len(values) else values[i]
                for i in range(0, len(values), 2)
            ]
        total = jnp.broadcast_to(
            jnp.sum(values[0], axis=1, keepdims=True), values[0].shape
        )
        return [total[j : j + 1] for j in range(count)]

    def red_drain(which):
        if n_peer > 1:
            red_all(which).wait_send()

    lane = lax.broadcasted_iota(jnp.int32, (span_y, nz), 1)
    first_lane, last_lane = lane == 0, lane == nz - 1

    def next_z(v):
        return pltpu.roll(v, nz - 1, 1)

    def prior_z(v):
        return jnp.where(first_lane, 0.0, pltpu.roll(v, 1, 1))

    def prior_y(v):
        return v + pltpu.roll(v, 1, 0)

    def span(margin):
        if n_gx == 1:
            return h, nx
        if n_gx == 2:
            return h - margin * gx, nx + margin
        return h - margin, nx + 2 * margin

    def apply(src, emit, margin):
        low, count = span(margin)

        def load(e):
            c = win(src, e)
            return c, next_z(c)

        def box(c, up):
            d = c + jnp.where(last_lane, 0.0, up)
            return d + pltpu.roll(d, span_y - 1, 0)

        before, before_up = load(low - 1)
        here, here_up = load(low)
        after, after_up = load(low + 1)
        box_b, box_h = box(before, before_up), box(here, here_up)
        g = win(k_b, low - 1) * (box_b + box_h)
        q = win(cx_b, low - 1) * before

        def body(t, carry):
            g_b, q_b, c, up, bx, c1, up1 = carry
            e = low + t
            c2, up2 = load(e + 2)
            bx1 = box(c1, up1)
            g = win(k_b, e) * (bx + bx1)
            gy_ = prior_y(g + g_b)
            cx, cz = win(cx_b, e), win(cz_b, e)
            t0 = (
                win(s8_b, e) * c
                + win(cy_b, e) * win(src, e, 1)
                + win(cy_b, e, -1) * win(src, e, -1)
                + cz * up
                + (cx * c1 + q_b)
                - gy_
            )
            emit(e, c, t0 + prior_z(cz * c - gy_))
            return g, cx * c, c1, up1, bx1, c2, up2

        loop(count, body, (g, q, here, here_up, box_h, after, after_up))

    def over(margin, body, unroll=True):
        low, count = span(margin)

        def step(t, carry):
            body(low + t)
            return carry

        loop(count, step, unroll=unroll)

    def own_copy(dst, src):
        def body(i, carry):
            dst[h + i, own_c] = src[h + i, own_c]
            return carry

        loop(nx, body)

    def moments(v, m, shift):
        zero = jnp.zeros((ny, nz), F32)

        def body(i, sums):
            diag = shift + 4.0 * s8_b[h + i, own_c]
            x = [v[k][h + i, own_c] for k in range(m + 1)]
            got = []
            for k in range(m):
                weighted = diag * x[k]
                got += [weighted * x[k], weighted * x[k + 1]]
            return tuple(s + g for s, g in zip(sums, got))

        return loop(nx, body, (zero,) * (2 * m))

    def krylov(v, m, inv_b, which, shift, after=None):
        for k in range(m):

            def emit(e, c, t):
                put(v[k + 1], e, win(inv_b, e) * t)

            apply(v[k], emit, m - 1 - k)
            if after is not None and k + 1 < m:
                after(k)
        red_start(which, moments(v, m, shift))
        if after is not None:
            after(m - 1)

    def galerkin(nu, m):
        a = [nu[j] + nu[j + 1] for j in range(2 * m - 1)]
        lower = [[None] * m for _ in range(m)]
        inverse, y = [], []
        for i in range(m):
            row = []
            for j in range(i):
                value = a[i + j]
                for q in range(j):
                    value = value - row[q] * lower[j][q]
                row.append(value)
                lower[i][j] = value * inverse[j]
            pivot, rhs = a[2 * i], nu[i]
            for q in range(i):
                pivot = pivot - row[q] * lower[i][q]
                rhs = rhs - lower[i][q] * y[q]
            good = pivot > 0.0
            inverse.append(jnp.where(good, 1.0 / jnp.where(good, pivot, 1.0), 0.0))
            y.append(rhs)
        c = [None] * m
        for i in reversed(range(m)):
            value = y[i] * inverse[i]
            for q in range(i + 1, m):
                value = value - lower[q][i] * c[q]
            c[i] = value
        return c

    def spread(values, n=None):
        n = span_y if n is None else n
        return [jnp.broadcast_to(v, (n, nz)) for v in values]

    def combine(c, x):
        m = len(c)
        w = c[0] * x[0]
        for k in range(1, m):
            w = w + c[k] * x[k]
        both = [c[0]] + [c[k - 1] + c[k] for k in range(1, m)] + [c[m - 1]]
        sh = both[0] * x[0]
        for k in range(1, m + 1):
            sh = sh + both[k] * x[k]
        return w, sh

    zero_row = jnp.zeros((wide, nz), F32)
    sources = [v.at[k] for v in (vf, vg) for k in range(MF)]
    sources += [vc.at[k] for k in range(ML)]
    sources += [vs.at[(ML + 1) * n + k] for n in range(stages) for k in range(ML)]
    for ref in sources:
        ref[h - 1] = zero_row
        ref[h + nx] = zero_row
    clear_strips(
        [xf.at[k] for k in range(MF)]
        + [xg.at[k] for k in range(MF)]
        + [xs.at[k] for k in range(ML * inner)]
        + [ab.at[k] for k in range(2 * inner)],
        0.0,
        F32,
    )
    regions = rigidity.shape[0]
    kel_of = [rigidity[r] * (1.0 / 12.0) for r in range(regions)]
    kal_of = [kel_of[r] * mismatch[r] for r in range(regions)]
    wide_lane = lax.broadcasted_iota(jnp.int32, (wide, nz), 1)
    node_y = gy * ny - PAD + SIDE + lax.broadcasted_iota(jnp.int32, (span_y, nz), 0)
    inside_y = (node_y >= 0) & (node_y < n_gy * ny)

    halo_wait(m_lab)
    low_e, count_e = span(MF)

    def lookup(e):
        ids = lab_x[e]
        kel = jnp.zeros((wide, nz), F32)
        kal = jnp.zeros((wide, nz), F32)
        for region in range(regions):
            here = ids == region
            kel = jnp.where(here, kel_of[region], kel)
            kal = jnp.where(here, kal_of[region], kal)
        k_b[e] = kel
        kal_b[e] = kal
        kz_b[e] = kel + jnp.where(wide_lane == 0, 0.0, pltpu.roll(kel, 1, 1))

    def nodal(e):
        kz = win(kz_b, e)
        kyz = kz + win(kz_b, e, -1)
        ky = win(k_b, e) + win(k_b, e, -1)
        kal = win(kal_b, e) + win(kal_b, e, -1)
        put(cx_b, e, kyz)
        return kyz, kz, ky, prior_z(kal) - kal

    lookup(low_e - 1)
    lookup(low_e)

    def setup(t, carry):
        e = low_e + t
        lookup(e)
        new = nodal(e)
        s8 = carry[0] + new[0]
        put(s8_b, e, s8)
        put(cy_b, e, carry[1] + new[1])
        put(cz_b, e, jnp.where(last_lane, 0.0, carry[2] + new[2]))
        put(theta_b, e, 3.0 * (carry[3] + new[3]))
        node_x = gx * nx - h + e
        inside = inside_y & (node_x >= 0) & (node_x < n_gx * nx)
        diag = 4.0 * s8
        put(ef_b, e, jnp.where(inside, 1.0 / (s_f + diag), 0.0))
        put(el_b, e, jnp.where(inside, 1.0 / (s_l + diag), 0.0))
        return new

    loop(count_e, setup, nodal(low_e - 1))

    @pl.when((tm > 0) & (tm == n_tm - 2))
    def _():
        heat_relay()

    u0_x, h1_x = in_x.at[U0 - 1], in_x.at[H1 - 1]
    hist_x = [in_x.at[HIST - 1 + p] for p in prods]
    halo_wait(m_u0, m_h1)

    def first_level(e, c, t):
        image = t + 4.0 * win(s8_b, e) * c
        put(au_b, e, image)
        r = gain_f * c + heat_f[0] * win(theta_b, e) + win(h1_x, e) - image
        put(vf.at[0], e, win(ef_b, e) * r)

    apply(u0_x, first_level, MF)

    def sender(x, v, messages):
        def after(k):
            own_copy(x.at[k], v[k + 1])
            halo_start(messages[k])

        return after

    vf_ = [vf.at[k] for k in range(MF + 1)]
    vg_ = [vg.at[k] for k in range(MF + 1)]
    vc_ = [vc.at[k] for k in range(ML + 1)]
    xf_ = [vf.at[0]] + [xf.at[k] for k in range(MF)]
    xg_ = [vg.at[0]] + [xg.at[k] for k in range(MF)]
    krylov(vf_, MF, ef_b, R_FINE1, s_f, sender(xf, vf_, m_xf))

    halo_wait(m_hd)
    hd_x, hc_x = in_x.at[HD - 1], in_x.at[HC - 1]

    def base_fine2(e):
        r = heat_f[1] * win(theta_b, e) - held * win(u0_x, e) - win(au_b, e)
        put(rb_b, e, r + win(hd_x, e))

    over(MF, base_fine2)

    @pl.when(first_plane)
    def _():
        halo_start(*m_hist)

    @pl.when((tm > 0) & (tm < n_tm - 2))
    def _():
        heat_relay()

    if inner:

        @pl.when((tm > 0) & (tm < stages))
        def _():
            pl.semaphore_wait(token, 1)

        @pl.when((tm > 0) & (tm < stages - 1))
        def _():
            pl.semaphore_signal(
                token, inc=1, device_id=(tm + 1, gx, gy), device_id_type=MESH
            )

    @pl.when(tm > 0)
    def _():
        halo_wait(m_hc)

        def coarse_first(e):
            r = gain_l * win(u0_x, e) + heat_l * win(theta_b, e) - win(au_b, e)
            r = r + win(hc_x, e)
            put(vc.at[0], e, win(el_b, e) * r)

        over(ML, coarse_first)
        krylov(vc_, ML, el_b, R_COARSE, s_l)

    c1 = galerkin(red_finish(R_FINE1, 2 * MF), MF)
    c1w = spread(c1)
    halo_wait(*m_xf)
    lift_f = s_f - held

    def second_level(e):
        w, sh = combine(c1w, [win(x, e) for x in xf_])
        put(vg.at[0], e, win(ef_b, e) * (win(rb_b, e) + lift_f * w) - sh)

    over(MF, second_level)

    @pl.when(first_plane)
    def _():
        krylov(vg_, MF, ef_b, R_FINE2, s_f, sender(xg, vg_, m_xg))

        def after_fine1(e):
            w, sh = combine(c1w, [win(x, e) for x in xf_])
            u = win(u0_x, e) + w
            image = win(au_b, e) + (s_f + 4.0 * win(s8_b, e)) * sh - s_f * w
            put(u_b, e, u)
            put(au_b, e, image)
            r = (gain_l + kappa_f) * u - image
            for p in prods:
                past = d_l[p] * win(hist_x[p], e) + (d_f[p] * keep_f[p]) * u
                put(hb.at[p], e, past)
                r = r + f_l[p] * past
            put(rb_b, e, r)

        halo_wait(*m_hist)
        over(ML, after_fine1)

        def keep_u1(i, carry):
            own_ab[1, i] = u_b[h + i, own_c]
            return carry

        loop(nx, keep_u1)
        up_copy(prony + 1, True).start()
        heat_copy().wait_recv()

        def add_heat(e):
            put(rb_b, e, win(rb_b, e) + heat_in[0, 0:1] * win(theta_b, e))

        over(ML, add_heat)

        c2w = spread(galerkin(red_finish(R_FINE2, 2 * MF), MF))
        halo_wait(*m_xg)
        lift = gain_l + kappa_f + s_f

        def v_of(n):
            return [vs.at[(ML + 1) * (n - 1) + k] for k in range(ML + 1)]

        def x_of(n):
            return [v_of(n)[0]] + [xs.at[ML * (n - 1) + k] for k in range(ML)]

        def stage_start(n):
            v = v_of(n)
            after = None
            if n < stages:
                after = sender(xs.at[pl.ds(ML * (n - 1), ML)], v, m_xs(n))
            krylov(v, ML, el_b, R_STAGE + n - 1, s_l, after)

        def stage1_level(e):
            w, sh = combine(c2w, [win(x, e) for x in xg_])
            r = win(rb_b, e) + lift * w - (s_f + 4.0 * win(s8_b, e)) * sh
            put(v_of(1)[0], e, win(el_b, e) * r)

        over(ML, stage1_level)
        stage_start(1)

        def after_fine2(e):
            w, sh = combine(c2w, [win(x, e) for x in xg_])
            u = win(u_b, e) + w
            put(u_b, e, u)
            image = win(au_b, e) + (s_f + 4.0 * win(s8_b, e)) * sh - s_f * w
            put(au_b, e, image)
            for p in prods:
                put(hb.at[p], e, win(hb.at[p], e) + keep_f[p] * u)

        over(ML, after_fine2)

        def first_out(i, carry):
            u = u_b[h + i, own_c]
            own_ab[0, i] = u
            out[0, 0, i] = u
            for p in prods:
                out[0, 1 + p, i] = hb[p, h + i, own_c]
            return carry

        loop(nx, first_out)
        up_copy(prony, True).start()

        rise = gain_l + kappa_l + s_l
        for n in range(1, stages):
            a_x, b_x = ab.at[2 * (n - 1)], ab.at[2 * (n - 1) + 1]
            give_each(n, 1, -1, lambda c: c.wait_recv())
            give_each(n, 0, -1, lambda c: c.wait_recv())

            def correction(e, c, t):
                put(aa_b, e, t + 4.0 * win(s8_b, e) * c)

            apply(a_x, correction, ML)

            def base_stage(e):
                a, b, u = win(a_x, e), win(b_x, e), win(u_b, e)
                r = gain_l * (u + a) - win(au_b, e) - win(aa_b, e)
                r = r + kappa_l * u + kappa_f * a
                r = r + heat_in[n, 0:1] * win(theta_b, e)
                for p in prods:
                    past = d_l[p] * win(hb.at[p], e) + (d_f[p] * keep_f[p]) * b
                    r = r + f_l[p] * past
                put(rb_b, e, r)

            over(ML, base_stage)
            cw = spread(galerkin(red_finish(R_STAGE + n - 1, 2 * ML), ML))
            halo_wait(*m_xs(n))

            def stage_level(e):
                w, sh = combine(cw, [win(x, e) for x in x_of(n)])
                r = win(rb_b, e) + rise * w
                put(v_of(n + 1)[0], e, win(el_b, e) * r - sh)

            over(ML, stage_level)
            stage_start(n + 1)

            def after_stage(e):
                w, sh = combine(cw, [win(x, e) for x in x_of(n)])
                moved = win(u_b, e) + w
                a, b = win(a_x, e), win(b_x, e)
                put(u_b, e, moved + a)
                image = win(au_b, e) + (s_l + 4.0 * win(s8_b, e)) * sh - s_l * w
                put(au_b, e, image + win(aa_b, e))
                for p in prods:
                    past = d_l[p] * win(hb.at[p], e) + keep_l[p] * moved
                    put(hb.at[p], e, past + keep_f[p] * (a + d_f[p] * b))

            over(ML, after_stage)

            def stage_out(i, carry):
                gu_out[n - 1, i] = u_b[h + i, own_c] - a_x[h + i, own_c]
                return carry

            loop(nx, stage_out)
            for to in range(n, n_tm):
                for copy in z_copies(n, to):
                    copy.start()

        v = v_of(stages)
        c = galerkin(red_finish(R_STAGE + stages - 1, 2 * ML), ML)
        cw = spread(c, ny)
        for index, (start, count) in enumerate(chunks):

            def last_stage(i, carry):
                e = h + start + i
                u = u_b[e, own_c]
                for k in range(ML):
                    u = u + cw[k] * v[k][e, own_c]
                gu_out[stages - 1, start + i] = u
                return carry

            loop(count, last_stage)
            z_copies(stages, stages)[index].start()

        halo_drain(*m_xg)
        for n in range(1, stages):
            halo_drain(*m_xs(n))
        for n in range(stages):
            red_drain(R_STAGE + n)
        for j in range(1, n_tm):
            for to in range(j, n_tm):
                for copy in z_copies(j, to):
                    copy.wait_send()
        for item in range(prony + 2):
            up_copy(item, True).wait_send()
        halo_drain(*m_hist)

    @pl.when(tm > 0)
    def _():
        krylov(vg_, MF, ef_b, R_FINE2, s_f)
        c1o = spread(c1, ny)
        cco = spread(galerkin(red_finish(R_COARSE, 2 * ML), ML), ny)

        def early(i, carry):
            e = h + i
            b = c1o[0] * vf[0, e, own_c]
            for k in range(1, MF):
                b = b + c1o[k] * vf[k, e, own_c]
            for k in range(ML):
                b = b - cco[k] * vc[k, e, own_c]
            own_ab[1, i] = b
            return carry

        loop(nx, early)
        give(1, lambda c: c.start())

        c2o = spread(galerkin(red_finish(R_FINE2, 2 * MF), MF), ny)

        def late(i, carry):
            e = h + i
            b = own_ab[1, i]
            a = b
            for k in range(MF):
                a = a + c2o[k] * vg[k, e, own_c]
            own_ab[0, i] = a
            return carry

        loop(nx, late)
        give(0, lambda c: c.start())

        def carry_on(i, past):
            a, b = own_ab[0, i], own_ab[1, i]
            for p in prods:
                value = d_l[p] * past[p] + keep_f[p] * (a + d_f[p] * b)
                y_out[p, i] = value
                out[0, 1 + p, i] = value

        for p in prods:
            up_copy(p, True).wait_recv()

        @pl.when(tm == 1)
        def _():
            for f in range(2):
                up_copy(prony + f, True).wait_recv()

            def body(i, carry):
                u1, u2 = first_in[1, i], first_in[0, i]
                past = [
                    d_l[p] * y_in[p, i] + keep_f[p] * (u2 + d_f[p] * u1) for p in prods
                ]
                carry_on(i, past)
                return carry

            loop(nx, body)

        @pl.when(tm > 1)
        def _():
            def body(i, carry):
                carry_on(i, [y_in[p, i] for p in prods])
                return carry

            loop(nx, body)

        @pl.when(tm < n_tm - 1)
        def _():
            for p in prods:
                up_copy(p, False).start()

        for n in range(1, n_tm):

            @pl.when(tm == n)
            def _():
                for j in range(1, n):
                    for copy in z_copies(j, n):
                        copy.wait_recv()

                def before(i, carry):
                    for p in prods:
                        past = gu_in[0, i]
                        for j in range(2, n):
                            past = d_l[p] * past + gu_in[j - 1, i]
                        out[0, 1 + p, i] = out[0, 1 + p, i] + (d_l[p] * keep_l[p]) * past
                    return carry

                if n > 1:
                    loop(nx, before)
                for copy, (item, at) in zip(z_copies(n, n), z_items(n)):
                    copy.wait_recv()

                    def final_out(t, carry):
                        i = at.start + t
                        u = gu_in[n - 1, i]
                        out[0, 0, i] = u + own_ab[0, i]
                        for p in prods:
                            out[0, 1 + p, i] = out[0, 1 + p, i] + keep_l[p] * u
                        return carry

                    loop(at.size, final_out)

        @pl.when(tm < n_tm - 1)
        def _():
            for p in prods:
                up_copy(p, False).wait_send()

        red_drain(R_COARSE)
        heat_copy().wait_send()
        halo_drain(m_hc)
        for f in range(2):
            give(f, lambda c: c.wait_send())

    halo_drain(m_lab, m_u0, m_h1, m_hd, *m_xf)
    red_drain(R_FINE1)
    red_drain(R_FINE2)


def on_device(sizes, state, labels, rigidity, mismatch, heat, coefs, times):
    _, fields, nx, ny, nz = state.shape
    n_tm = sizes[0]
    stages = n_tm - 1
    inner = max(stages - 1, 1)
    prony = fields - 1
    rows, wide = nx + 2 * RIM + 2, ny + 2 * PAD
    peers = sizes[1] * sizes[2]
    field = (rows, wide, nz)
    own = (nx, ny, nz)
    vmem = pl.BlockSpec(memory_space=pltpu.VMEM)
    smem = pl.BlockSpec(memory_space=pltpu.SMEM)
    dma = pltpu.SemaphoreType.DMA
    reds = R_STAGE + stages
    messages = HIST + prony + 2 * MF + (ML + 2) * inner
    items = stages - 1 + len(chunks_of(nx))

    def vm(*shape):
        return pltpu.VMEM(shape, F32)

    return pl.pallas_call(
        functools.partial(kernel, sizes),
        out_shape=jax.ShapeDtypeStruct(state.shape, state.dtype),
        in_specs=[vmem, vmem, smem, smem, smem, smem, smem],
        out_specs=vmem,
        scratch_shapes=[pltpu.VMEM(field, jnp.int32), vm(4 + prony, *field)]
        + [vm(*field) for _ in range(10)]
        + [
            vm(MF + 1, *field),
            vm(MF + 1, *field),
            vm(ML + 1, *field),
            vm((ML + 1) * stages, *field),
            vm(MF, *field),
            vm(MF, *field),
            vm(ML * inner, *field),
            vm(2 * inner, *field),
            vm(*field),
            vm(*field),
            vm(*field),
            vm(*field),
            vm(prony, *field),
            vm(2, *own),
            vm(stages, *own),
            vm(stages, *own),
            vm(prony, *own),
            vm(prony, *own),
            vm(2, *own),
            vm(stages, 8, nz),
            vm(stages, 8, nz),
            vm(reds, 8, nz),
            vm(reds, max(peers - 1, 1), 8, nz),
            dma((messages, 9)),
            dma((messages, 9)),
            dma((reds,)),
            dma((reds,)),
            dma((stages, items)),
            dma((items,)),
            dma((prony + 2,)),
            dma((prony + 2,)),
            dma,
            dma,
            pltpu.SemaphoreType.REGULAR,
        ],
        compiler_params=pltpu.CompilerParams(
            collective_id=0, has_side_effects=True, vmem_limit_bytes=56 * 1024 * 1024
        ),
    )(state, labels, rigidity, mismatch, heat, coefs, times)


def solution(mesh):
    sizes = tuple(mesh.shape[name] for name in ("tm", "gx", "gy"))
    placed = (
        P("tm", None, "gx", "gy", None),
        P("gx", "gy", None),
        P(),
        P(),
        P("tm", None),
        P(),
        P(),
    )
    return jax.shard_map(
        functools.partial(on_device, sizes),
        mesh=mesh,
        in_specs=placed,
        out_specs=P("tm", None, "gx", "gy", None),
        check_vma=False,
    )
```

time: 59.9 us -> 54.9 us (0.917)
  the two profiles are of different devices: /device:TPU:25 before, /device:TPU:0 now
where the time goes in v1:
time: 54.9 us; the launch traced here: 54.7 us
  Pallas kernels  52.9 us (96%)
  local copies, waits for them, and re-layouts  1.77 us (3%)
    pallas_call x1, Pallas kernels, on_device(): pl.pallas_call(functools.partial(kernel, sizes), out_shape=jax.ShapeDtype...  52.9 us
    unnamed x1, local copies, waits for them, and re-layouts  1.77 us

profile of v1, /device:TPU:0, one launch (start us, length us, event | category | flops | bytes accessed | tf_op | source)
XLA Modules:
  0.0 54.7 jit_solution(13900341388705840017)
XLA Ops:
  0.0 52.9 %shard_map.73 = f32[1,4,12,16,128]{4,3,2,1,0:T(8,128)} custom-call(f32[1,4,12,16,128]{4,3,2,1,0:T(8,128)} %state.1, s32[12,16,128]{2,1,0:T(8,128)} %labels.1, f32[6]{0:T(128)} %rigidity.1, f32[6]{0:T(128)} %mismatch.1, f32[1,2]{1,0:T(1,128)} %heat.1, f32[3]{0:T(128)} %coefs.1, f32[3]{0:T(128)} %times.1), custom_call_target="tpu_custom_call" | custom-call | tf_op jit(solution)/shard_map/pallas_call | solution.py:997
  53.0 1.8 %copy.9 = f32[1,4,12,16,128]{4,3,2,1,0:T(8,128)} copy(f32[1,4,12,16,128]{4,3,2,1,0:T(8,128)} %shard_map.73) | data formatting | bytes 786432
